TPU v7x, 256 devices: a whole 4x4x8 slice. The times are simulated.
256 devices in a mesh: seq: 64 (over y, z, x_hi), tp: 4 (over x_lo, core).
Axes of the slice: x: 4 (x_hi: 2, x_lo: 2; x = x_hi * 2 + x_lo), y: 4, z: 8, core: 2. Of those that a mesh axis runs over, the one named last changes fastest.
Arguments:
- query_input: bfloat16 [8192, 4096], P('seq', 'tp'), may hold values from -6 to 6
- key_input: bfloat16 [8192, 4096], P('seq', 'tp'), may hold values from -6 to 6
- value_input: bfloat16 [8192, 4096], P('seq', 'tp'), may hold values from -6 to 6
- short_filter: float32 [3, 3, 4096], P(None, None, 'tp'), may hold values from -3 to 3
- residues: float32 [16, 4096], P(None, 'tp'), may hold values from -1.5 to 1.5
- decays: float32 [16, 4096], P(None, 'tp'), as said below
- skip_gain: float32 [4096], P('tp'), may hold values from -4 to 4
- head_weight: bfloat16 [32, 4096, 128], P(None, ('tp', 'seq')), may hold values from -0.015625 to 0.015625
Outputs:
- operator_out: bfloat16 [8192, 4096], P('seq', 'tp')
- probe_out: bfloat16 [512, 128], P(('seq', 'tp'))
Inputs may be any that keep to these rules, and one draw needn't show every extreme that they name: `decays`: each rate is positive, at least 1 / 16384 and at most 1 / 30.
All inputs are finite; a program needn't handle non-finite values.
Results may differ from a plain program's by a relative error of at most 0.01.
Values may be sent and summed in bfloat16 or wider, within the bound.
No kernel may reach another device: no remote copies, remote signals or barrier semaphores. Data moves between devices by JAX's collectives and lax.ppermute only.
A program may use at most 64 MiB of HBM per device.

v0:
```python
import jax
import jax.numpy as jnp
from jax import lax
from jax.sharding import PartitionSpec as P

STRIDE = 16
CHUNK = 128
highest = lax.Precision.HIGHEST


def from_behind(block, axis, distance):
    devices = range(lax.axis_size(axis))
    route = [(i - distance, i) for i in devices if i - distance in devices]
    return lax.ppermute(block, axis, route)


def short_pass(rows, before, tap_weights):
    joined = jnp.concatenate([before, rows], axis=0).astype(jnp.float32)
    row_count = rows.shape[0]
    return (
        tap_weights[0] * joined[2 : 2 + row_count]
        + tap_weights[1] * joined[1 : 1 + row_count]
        + tap_weights[2] * joined[0:row_count]
    )


def modal_conv(gated, residues, decays):
    span, width = gated.shape
    chunks = span // CHUNK
    groups = lax.axis_size("u")
    g = gated.astype(jnp.float32).reshape(chunks, CHUNK, width)
    steps = jnp.arange(CHUNK, dtype=jnp.float32)
    weight = residues * jnp.sqrt(-jnp.expm1(-2.0 * decays))
    grow = jnp.exp(decays[:, None, :] * steps[None, :, None])
    shrink = jnp.exp(-decays[:, None, :] * steps[None, :, None])
    lower = (steps[:, None] >= steps[None, :]).astype(jnp.float32)
    running = jnp.einsum("ij,rkjc->rkic", lower, grow[:, None] * g[None], precision=highest)
    ends = jnp.exp(-decays * (CHUNK - 1))[:, None, :] * running[:, :, -1, :]
    index = jnp.arange(chunks)
    lag = (index[:, None] - 1 - index[None, :]).astype(jnp.float32)
    decay_table = jnp.where(
        (lag >= 0)[None, :, :, None],
        jnp.exp(-decays[:, None, None, :] * (CHUNK * jnp.maximum(lag, 0.0))[None, :, :, None]),
        0.0,
    )
    inner = jnp.sum(decay_table * ends[:, None, :, :], axis=2)
    total = jnp.exp(-decays * CHUNK) * inner[:, -1] + ends[:, -1]
    outer = None
    for m in range(1, groups):
        term = from_behind(total, "u", m)
        if m > 1:
            term = jnp.exp(-decays * float(span * (m - 1))) * term
        outer = term if outer is None else outer + term
    if outer is not None:
        offsets = (CHUNK * index).astype(jnp.float32)
        inner = inner + jnp.exp(-decays[:, None, :] * offsets[None, :, None]) * outer[:, None, :]
    after = jnp.exp(-decays[:, None, :] * (steps[None, :, None] + 1.0))
    modes = shrink[:, None] * running + after[:, None] * inner[:, :, None, :]
    return jnp.sum(weight[:, None, None, :] * modes, axis=0).reshape(span, width)


def shards(
    query_input, key_input, value_input, short_filter, residues, decays, skip_gain, head_weight
):
    tokens, chan_width = query_input.shape
    width_u = lax.axis_size("u")
    width_v = lax.axis_size("v")
    piece = head_weight.shape[1]
    span = tokens * width_v
    narrow = width_u * piece
    stacked = jnp.stack([query_input, key_input, value_input], axis=0)
    stacked = stacked.reshape(1, 3, tokens, width_u, width_v, piece)
    columns = lax.all_to_all(stacked, "v", split_axis=4, concat_axis=0, tiled=True)
    columns = columns.reshape(width_v, 3, tokens, narrow)
    columns = jnp.transpose(columns, (1, 0, 2, 3)).reshape(3, span, narrow)
    weight_rep = jnp.broadcast_to(head_weight[None], (width_u,) + head_weight.shape)
    weight_cols = lax.all_to_all(weight_rep, "u", split_axis=0, concat_axis=0, tiled=True)
    weight_cols = jnp.transpose(weight_cols, (1, 0, 2, 3)).reshape(
        head_weight.shape[0], narrow, head_weight.shape[2]
    )
    before = from_behind(columns[:, -2:], "u", 1)
    sf = short_filter.reshape(3, 3, width_u, width_v, piece)
    sf = jnp.transpose(sf, (0, 1, 3, 2, 4))
    sf = lax.dynamic_index_in_dim(sf, lax.axis_index("v"), axis=2, keepdims=False)
    sf = sf.reshape(3, 3, narrow)

    def pick(values):
        shaped = values.reshape(values.shape[0], width_u, width_v, piece)
        shaped = lax.dynamic_index_in_dim(shaped, lax.axis_index("v"), axis=2, keepdims=False)
        return shaped.reshape(values.shape[0], narrow)

    query_short = short_pass(columns[0], before[0], sf[:, 0])
    key_short = short_pass(columns[1], before[1], sf[:, 1])
    value_short = short_pass(columns[2], before[2], sf[:, 2])
    gated = (key_short * value_short).astype(jnp.bfloat16)
    convolved = modal_conv(gated, pick(residues), pick(decays))
    gain = pick(skip_gain[None])[0]
    carried = (convolved + gain * gated.astype(jnp.float32)).astype(jnp.bfloat16)
    op_cols = (query_short * carried.astype(jnp.float32)).astype(jnp.bfloat16)
    back = op_cols.reshape(width_v, tokens, width_u, 1, piece)
    back = lax.all_to_all(back, "v", split_axis=0, concat_axis=3, tiled=True)
    operator_out = back.reshape(tokens, chan_width)
    rim_rows = from_behind(op_cols[:STRIDE], "u", -1)
    extended = jnp.concatenate([op_cols, rim_rows], axis=0)
    rows = span // STRIDE
    early_rows = extended[:span].reshape(rows, STRIDE, narrow)
    late_rows = extended[STRIDE:].reshape(rows, STRIDE, narrow)
    running = jnp.einsum(
        "jic,ico->jo", early_rows, weight_cols[:STRIDE], preferred_element_type=jnp.float32
    )
    partial_sum = running + jnp.einsum(
        "jic,ico->jo", late_rows, weight_cols[STRIDE:], preferred_element_type=jnp.float32
    )
    partial_sum = partial_sum.reshape(width_v, rows // width_v, -1)
    partial_sum = lax.all_to_all(partial_sum, "v", split_axis=0, concat_axis=0, tiled=True)
    block_sum = jnp.sum(partial_sum, axis=0)
    probe_out = lax.psum_scatter(block_sum, "tp", scatter_dimension=0, tiled=True).astype(
        jnp.bfloat16
    )
    return (operator_out, probe_out)


def solution(mesh):
    seq_size, tp_size = mesh.devices.shape
    width_u = 4 if seq_size % 4 == 0 else 1
    split = jax.sharding.Mesh(
        mesh.devices.reshape(width_u, seq_size // width_u, tp_size), ("u", "v", "tp")
    )
    seq = ("u", "v")
    placed = (
        P(seq, "tp"),
        P(seq, "tp"),
        P(seq, "tp"),
        P(None, None, "tp"),
        P(None, "tp"),
        P(None, "tp"),
        P("tp"),
        P(None, ("tp", "u", "v"), None),
    )
    return jax.shard_map(
        shards,
        mesh=split,
        in_specs=placed,
        out_specs=(P(seq, "tp"), P(("u", "v", "tp"), None)),
        check_vma=False,
    )
```

profile of v0, /device:TPU:16, one launch (start us, length us, event | category | flops | bytes accessed | tf_op | source)
XLA Modules:
  0.0 130.6 jit_solution(3539531333170131644)
XLA Ops:
  0.6 1.2 copy.108
  1.8 1.1 copy.107
  2.9 1.1 copy.106
  5.3 11.0 %all-to-all-start = ((bf16[1,3,128,4,16,16]{2,5,3,1,0,4:T(8,128)(2,1)}), bf16[1,3,128,4,16,16]{2,5,3,1,0,4:T(8,128)(2,1)S(1)}, u32[]{:S(2)}, u32[]{:S(2)}) async-start(bf16[1,3,128,4,16,16]{2,5,3,1,0,4:T(8,128)(2,1)} %copy.109), calls=%async_computation | async-start | bytes 1572864 | tf_op jit(solution)/shard_map/all_to_all | solution.py:73
  20.4 20.5 %all-to-all-done = bf16[1,3,128,4,16,16]{2,5,3,1,0,4:T(8,128)(2,1)S(1)} async-done(((bf16[1,3,128,4,16,16]{2,5,3,1,0,4:T(8,128)(2,1)}), bf16[1,3,128,4,16,16]{2,5,3,1,0,4:T(8,128)(2,1)S(1)}, u32[]{:S(2)}, u32[]{:S(2)}) %all-to-all-start) | async-done | bytes 786464 | tf_op jit(solution)/shard_map/all_to_all | solution.py:73
  41.8 4.8 %all-to-all-start.2 = ((bf16[4,32,16,128]{3,2,1,0:T(8,128)(2,1)}), bf16[4,32,16,128]{3,2,1,0:T(8,128)(2,1)S(1)}, u32[]{:S(2)}, u32[]{:S(2)}) async-start(bf16[4,32,16,128]{3,2,1,0:T(8,128)(2,1)} %broadcast_in_dim.12), calls=%async_computation.2 | async-start | bytes 1048576 | tf_op jit(solution)/shard_map/all_to_all | solution.py:77
  46.9 3.3 %collective-permute-start = (bf16[3,2,64]{1,2,0:T(8,128)(2,1)S(1)}, bf16[3,2,64]{1,2,0:T(8,128)(2,1)S(1)}, u32[]{:S(2)}, u32[]{:S(2)}) collective-permute-start(bf16[3,2,64]{1,2,0:T(8,128)(2,1)S(1)} %slice.161), channel_id=1, source_target_pairs={{0,64},{64,128},{128,192},{1,65},{65,129},{129,193},{2,66},{66,130... | collective-permute-start | bytes 2312 | tf_op jit(solution)/shard_map/ppermute | solution.py:14
  51.0 1.9 %collective-permute-done = bf16[3,2,64]{1,2,0:T(8,128)(2,1)S(1)} collective-permute-done((bf16[3,2,64]{1,2,0:T(8,128)(2,1)S(1)}, bf16[3,2,64]{1,2,0:T(8,128)(2,1)S(1)}, u32[]{:S(2)}, u32[]{:S(2)}) %collective-permute-start) | collective-permute-done | bytes 800 | tf_op jit(solution)/shard_map/ppermute | solution.py:14
  54.0 4.2 %fusion.4 = f32[16,16,128,64]{2,3,1,0:T(8,128)S(1)} fusion(f32[16,128,64]{1,2,0:T(8,128)S(1)} %bitcast.121, f32[16,128,64]{1,2,0:T(8,128)S(1)} %multiply_exponential_fusion.1), kind=kOutput, calls=%fused_computation.5 | convolution fusion | flops 3223339008 | bytes 9437184 | tf_op jit(solution)/shard_map/ij,rkjc->rkic/dot_general | solution.py:37
  58.3 3.2 %copy-done = f32[16,16,128,64]{2,3,1,0:T(8,128)} copy-done((f32[16,16,128,64]{2,3,1,0:T(8,128)}, f32[16,16,128,64]{2,3,1,0:T(8,128)S(1)}, u32[]{:S(2)}) %copy-start) | copy-done | bytes 8388632
  61.5 5.5 %slice.185 = f32[16,16,1,64]{2,3,1,0:T(8,128)} slice(f32[16,16,128,64]{2,3,1,0:T(8,128)S(1)} %fusion.4), slice={[0:16], [0:16], [127:128], [0:64]} | slice | bytes 131072 | tf_op jit(solution)/shard_map/slice | solution.py:38
  67.0 5.4 %copy.139 = f32[16,16,1,64]{3,0,1,2:T(8,128)S(1)} copy(f32[16,16,1,64]{2,3,1,0:T(8,128)} %slice.185) | data formatting | bytes 131072 | tf_op jit(solution)/shard_map/squeeze | solution.py:38
  72.5 1.3 multiply_reduce_fusion.1
  74.4 3.7 %collective-permute-start.1 = (f32[16,64]{1,0:T(8,128)S(1)}, f32[16,64]{1,0:T(8,128)S(1)}, u32[]{:S(2)}, u32[]{:S(2)}) collective-permute-start(f32[16,64]{1,0:T(8,128)S(1)} %fusion.25), channel_id=1, source_target_pairs={{0,64},{64,128},{128,192},{1,65},{65,129},{129,193},{2,66},{66,130... | collective-permute-start | bytes 12296 | tf_op jit(solution)/shard_map/ppermute | solution.py:14
  78.2 1.3 collective-permute-start.2
  80.0 5.2 %collective-permute-done.2 = f32[16,64]{1,0:T(8,128)S(1)} collective-permute-done((f32[16,64]{1,0:T(8,128)S(1)}, f32[16,64]{1,0:T(8,128)S(1)}, u32[]{:S(2)}, u32[]{:S(2)}) %collective-permute-start.2) | collective-permute-done | bytes 4128 | tf_op jit(solution)/shard_map/ppermute | solution.py:14
  85.3 5.4 %multiply_reduce_fusion = f32[16,128,64]{1,2,0:T(8,128)S(1)} fusion(f32[16,16,128,64]{2,3,1,0:T(8,128)} %copy-done, f32[16,16,64]{2,1,0:T(8,128)S(1)} %multiply_add_fusion, f32[16,128,64]{1,2,0:T(8,128)S(1)} %get-tuple-element.26, f32[16,128,64]{1,2,0:T(8,128)S(1)} %get-tuple-element.25, f32[16,64]{1,0:T(8,128)S(1)} %get-tuple-element.22), kind=kLoop, calls=%fused_computation | loop fusion | flops 10354688 | bytes 10031104 | tf_op jit(solution)/shard_map/reduce_sum | solution.py:59
  91.2 1.9 %collective-permute-start.4 = (bf16[16,64]{0,1:T(8,128)(2,1)S(1)}, bf16[16,64]{0,1:T(8,128)(2,1)S(1)}, u32[]{:S(2)}, u32[]{:S(2)}) collective-permute-start(bf16[16,64]{0,1:T(8,128)(2,1)S(1)} %slice.189), channel_id=1, source_target_pairs={{64,0},{128,64},{192,128},{65,1},{129,65},{193,129},{66,2},{130,66... | collective-permute-start | bytes 6152 | tf_op jit(solution)/shard_map/ppermute | solution.py:14
  93.5 3.3 %collective-permute-done.4 = bf16[16,64]{0,1:T(8,128)(2,1)S(1)} collective-permute-done((bf16[16,64]{0,1:T(8,128)(2,1)S(1)}, bf16[16,64]{0,1:T(8,128)(2,1)S(1)}, u32[]{:S(2)}, u32[]{:S(2)}) %collective-permute-start.4) | collective-permute-done | bytes 2080 | tf_op jit(solution)/shard_map/ppermute | solution.py:14
  98.6 4.5 %all-to-all-start.3 = ((f32[16,8,128]{2,1,0:T(8,128)}), f32[16,8,128]{2,1,0:T(8,128)S(1)}, u32[]{:S(2)}, u32[]{:S(2)}) async-start(f32[16,8,128]{2,1,0:T(8,128)} %fusion.8), calls=%async_computation.3 | async-start | bytes 131072 | tf_op jit(solution)/shard_map/all_to_all | solution.py:115
  103.9 9.7 %all-to-all-done.3 = f32[16,8,128]{2,1,0:T(8,128)S(1)} async-done(((f32[16,8,128]{2,1,0:T(8,128)}), f32[16,8,128]{2,1,0:T(8,128)S(1)}, u32[]{:S(2)}, u32[]{:S(2)}) %all-to-all-start.3) | async-done | bytes 65568 | tf_op jit(solution)/shard_map/all_to_all | solution.py:115
  113.6 3.5 %all-to-all-start.1 = ((bf16[16,128,4,1,16]{1,4,2,3,0:T(8,128)(2,1)}), bf16[16,128,4,1,16]{1,4,2,3,0:T(8,128)(2,1)S(1)}, u32[]{:S(2)}, u32[]{:S(2)}) async-start(bf16[16,128,4,1,16]{1,4,2,3,0:T(8,128)(2,1)} %copy.126), calls=%async_computation.1 | async-start | bytes 524288 | tf_op jit(solution)/shard_map/all_to_all | solution.py:101
  118.5 6.0 %all-reduce = bf16[8,128]{1,0:T(8,128)(2,1)S(1)} all-reduce(f32[8,128]{1,0:T(8,128)S(1)} %reduce_sum.29), channel_id=2, replica_groups=mesh['u'=4,'v'=16,'tp'=4] {'tp'}, use_global_device_ids=true, to_apply=%region_3.4.clone | all-reduce | flops 1024 | bytes 6144
  125.0 4.7 %all-to-all-done.1 = bf16[16,128,4,1,16]{1,4,2,3,0:T(8,128)(2,1)S(1)} async-done(((bf16[16,128,4,1,16]{1,4,2,3,0:T(8,128)(2,1)}), bf16[16,128,4,1,16]{1,4,2,3,0:T(8,128)(2,1)S(1)}, u32[]{:S(2)}, u32[]{:S(2)}) %all-to-all-start.1) | async-done | bytes 262176 | tf_op jit(solution)/shard_map/all_to_all | solution.py:101
  (71 shorter events, 15.0 us)
Async XLA Ops:
  0.6 40.3 %copy-start.1 = (bf16[32,16,128]{2,1,0:T(8,128)(2,1)S(1)}, bf16[32,16,128]{2,1,0:T(8,128)(2,1)}, u32[]{:S(2)}) copy-start(bf16[32,16,128]{2,1,0:T(8,128)(2,1)} %param.15) | copy-start | bytes 393220
  5.3 35.6 %all-to-all-start = ((bf16[1,3,128,4,16,16]{2,5,3,1,0,4:T(8,128)(2,1)}), bf16[1,3,128,4,16,16]{2,5,3,1,0,4:T(8,128)(2,1)S(1)}, u32[]{:S(2)}, u32[]{:S(2)}) async-start(bf16[1,3,128,4,16,16]{2,5,3,1,0,4:T(8,128)(2,1)} %copy.109), calls=%async_computation | async-start | bytes 1572864 | tf_op jit(solution)/shard_map/all_to_all | solution.py:73
  41.8 51.3 %all-to-all-start.2 = ((bf16[4,32,16,128]{3,2,1,0:T(8,128)(2,1)}), bf16[4,32,16,128]{3,2,1,0:T(8,128)(2,1)S(1)}, u32[]{:S(2)}, u32[]{:S(2)}) async-start(bf16[4,32,16,128]{3,2,1,0:T(8,128)(2,1)} %broadcast_in_dim.12), calls=%async_computation.2 | async-start | bytes 1048576 | tf_op jit(solution)/shard_map/all_to_all | solution.py:77
  46.9 6.0 %collective-permute-start = (bf16[3,2,64]{1,2,0:T(8,128)(2,1)S(1)}, bf16[3,2,64]{1,2,0:T(8,128)(2,1)S(1)}, u32[]{:S(2)}, u32[]{:S(2)}) collective-permute-start(bf16[3,2,64]{1,2,0:T(8,128)(2,1)S(1)} %slice.161), channel_id=1, source_target_pairs={{0,64},{64,128},{128,192},{1,65},{65,129},{129,193},{2,66},{66,130... | collective-permute-start | bytes 2312 | tf_op jit(solution)/shard_map/ppermute | solution.py:14
  58.3 3.2 %copy-start = (f32[16,16,128,64]{2,3,1,0:T(8,128)}, f32[16,16,128,64]{2,3,1,0:T(8,128)S(1)}, u32[]{:S(2)}) copy-start(f32[16,16,128,64]{2,3,1,0:T(8,128)S(1)} %fusion.4) | copy-start | bytes 25165828
  67.0 12.5 %copy-start.2 = (f32[1024]{0:T(1024)S(1)}, f32[1024]{0:T(1024)}, u32[]{:S(2)}) copy-start(f32[1024]{0:T(1024)} %param.14) | copy-start | bytes 12292
  73.8 5.9 %collective-permute-start.3 = (f32[16,64]{1,0:T(8,128)S(1)}, f32[16,64]{1,0:T(8,128)S(1)}, u32[]{:S(2)}, u32[]{:S(2)}) collective-permute-start(f32[16,64]{1,0:T(8,128)S(1)} %fusion.25), channel_id=1, source_target_pairs={{0,192},{1,193},{2,194},{3,195},{4,196},{5,197},{6,198},{7,199},{8... | collective-permute-start | bytes 12296 | tf_op jit(solution)/shard_map/ppermute | solution.py:14
  74.4 5.5 %collective-permute-start.1 = (f32[16,64]{1,0:T(8,128)S(1)}, f32[16,64]{1,0:T(8,128)S(1)}, u32[]{:S(2)}, u32[]{:S(2)}) collective-permute-start(f32[16,64]{1,0:T(8,128)S(1)} %fusion.25), channel_id=1, source_target_pairs={{0,64},{64,128},{128,192},{1,65},{65,129},{129,193},{2,66},{66,130... | collective-permute-start | bytes 12296 | tf_op jit(solution)/shard_map/ppermute | solution.py:14
  78.2 7.0 %collective-permute-start.2 = (f32[16,64]{1,0:T(8,128)S(1)}, f32[16,64]{1,0:T(8,128)S(1)}, u32[]{:S(2)}, u32[]{:S(2)}) collective-permute-start(f32[16,64]{1,0:T(8,128)S(1)} %fusion.25), channel_id=1, source_target_pairs={{0,128},{64,192},{1,129},{65,193},{2,130},{66,194},{3,131},{67,195... | collective-permute-start | bytes 12296 | tf_op jit(solution)/shard_map/ppermute | solution.py:14
  85.3 31.9 %copy-start.3 = (u32[256]{0:T(256)S(1)}, u32[256]{0:T(256)}, u32[]{:S(2)}) copy-start(u32[256]{0:T(256)} %constant.46) | copy-start | bytes 3076
  91.2 5.6 %collective-permute-start.4 = (bf16[16,64]{0,1:T(8,128)(2,1)S(1)}, bf16[16,64]{0,1:T(8,128)(2,1)S(1)}, u32[]{:S(2)}, u32[]{:S(2)}) collective-permute-start(bf16[16,64]{0,1:T(8,128)(2,1)S(1)} %slice.189), channel_id=1, source_target_pairs={{64,0},{128,64},{192,128},{65,1},{129,65},{193,129},{66,2},{130,66... | collective-permute-start | bytes 6152 | tf_op jit(solution)/shard_map/ppermute | solution.py:14
  98.6 15.1 %all-to-all-start.3 = ((f32[16,8,128]{2,1,0:T(8,128)}), f32[16,8,128]{2,1,0:T(8,128)S(1)}, u32[]{:S(2)}, u32[]{:S(2)}) async-start(f32[16,8,128]{2,1,0:T(8,128)} %fusion.8), calls=%async_computation.3 | async-start | bytes 131072 | tf_op jit(solution)/shard_map/all_to_all | solution.py:115
  113.6 16.1 %all-to-all-start.1 = ((bf16[16,128,4,1,16]{1,4,2,3,0:T(8,128)(2,1)}), bf16[16,128,4,1,16]{1,4,2,3,0:T(8,128)(2,1)S(1)}, u32[]{:S(2)}, u32[]{:S(2)}) async-start(bf16[16,128,4,1,16]{1,4,2,3,0:T(8,128)(2,1)} %copy.126), calls=%async_computation.1 | async-start | bytes 524288 | tf_op jit(solution)/shard_map/all_to_all | solution.py:101
where the time goes:
time: 131 us
  waiting for transfers between devices  45.7 us (35%)
  starting transfers between devices  34.7 us (26%)
  local copies, waits for them, and re-layouts  27.7 us (21%)
  other arithmetic  9.19 us (7%)
  blocking collectives  6 us (5%)
  matrix products  5.52 us (4%)
  between operations  1.74 us (1%)
    all_to_all x1, waiting for transfers between devices, shards(): lax.all_to_all(stacked, 'v', split_axis=4, concat_axis=0, tiled=True)  20.5 us
    all_to_all x1, starting transfers between devices, shards(): lax.all_to_all(stacked, 'v', split_axis=4, concat_axis=0, tiled=True)  11 us
    ppermute x5, starting transfers between devices, from_behind(): return lax.ppermute(block, axis, route)  10.8 us
    ppermute x5, waiting for transfers between devices, from_behind(): return lax.ppermute(block, axis, route)  10.7 us
    all_to_all x1, waiting for transfers between devices, shards(): lax.all_to_all(partial_sum, 'v', split_axis=0, concat_axis=0, tiled=True)  9.73 us
    unnamed x17, local copies, waits for them, and re-layouts  8.32 us
    unnamed x1, blocking collectives  6 us
    slice x1, local copies, waits for them, and re-layouts, modal_conv(): ends = jnp.exp(-decays * (CHUNK - 1))[:, None, :] * running[:, :, -1, :]  5.46 us
  transfers between devices with their start and end apart: 9, of which 7 were waited for; matrix products, arithmetic and copies ran while one was open for 24% of the time, Pallas kernels for 0%

commit v1 on v0

--- a/solution.py
+++ b/solution.py
@@ -6,6 +6,18 @@
 STRIDE = 16
 CHUNK = 128
 highest = lax.Precision.HIGHEST
+
+
+def recover_leaves_up(frame):
+    return jnp.concatenate(
+        lax.all_to_all(
+            jnp.stack(jnp.split(frame, lax.psum(1, "v"), 0)),
+            axis_name="v",
+            split_axis=0,
+            concat_axis=0,
+        ),
+        3,
+    )
 
 
 def from_behind(block, axis, distance):
@@ -98,7 +110,7 @@
     carried = (convolved + gain * gated.astype(jnp.float32)).astype(jnp.bfloat16)
     op_cols = (query_short * carried.astype(jnp.float32)).astype(jnp.bfloat16)
     back = op_cols.reshape(width_v, tokens, width_u, 1, piece)
-    back = lax.all_to_all(back, "v", split_axis=0, concat_axis=3, tiled=True)
+    back = recover_leaves_up(back)
     operator_out = back.reshape(tokens, chan_width)
     rim_rows = from_behind(op_cols[:STRIDE], "u", -1)
     extended = jnp.concatenate([op_cols, rim_rows], axis=0)

time: 131 us -> 137 us (1.046)
  local copies, waits for them, and re-layouts: 27.7 us -> 37.3 us
  waiting for transfers between devices: 45.7 us -> 41.1 us
    unnamed x17 -> x29, local copies, waits for them, and re-layouts: 8.32 us -> 17.4 us
    ppermute x5, waiting for transfers between devices: 10.7 us -> 7.51 us  [from_behind(): return lax.ppermute(block, axis, route)]
  transfers between devices with their start and end apart: 9 -> 9, of which waited for: 7 -> 6; matrix products, arithmetic and copies ran while one was open for 24% -> 25% of each run, Pallas kernels for 0% -> 0%
where the time goes in v1:
time: 137 us; the launch traced here: 136 us
  waiting for transfers between devices  41.1 us (30%)
  local copies, waits for them, and re-layouts  37.3 us (27%)
  starting transfers between devices  34.7 us (25%)
  other arithmetic  9.19 us (7%)
  blocking collectives  6.1 us (4%)
  matrix products  5.52 us (4%)
  between operations  1.76 us (1%)
    all_to_all x1, waiting for transfers between devices, shards(): lax.all_to_all(stacked, 'v', split_axis=4, concat_axis=0, tiled=True)  19.6 us
    unnamed x29, local copies, waits for them, and re-layouts  17.4 us
    all_to_all x1, starting transfers between devices, shards(): lax.all_to_all(stacked, 'v', split_axis=4, concat_axis=0, tiled=True)  11 us
    ppermute x5, starting transfers between devices, from_behind(): return lax.ppermute(block, axis, route)  10.8 us
    all_to_all x1, waiting for transfers between devices, shards(): lax.all_to_all(partial_sum, 'v', split_axis=0, concat_axis=0, tiled=True)  9.33 us
    ppermute x5, waiting for transfers between devices, from_behind(): return lax.ppermute(block, axis, route)  7.51 us
    unnamed x1, blocking collectives  6.1 us
    slice x1, local copies, waits for them, and re-layouts, modal_conv(): ends = jnp.exp(-decays * (CHUNK - 1))[:, None, :] * running[:, :, -1, :]  5.46 us
  transfers between devices with their start and end apart: 9, of which 6 were waited for; matrix products, arithmetic and copies ran while one was open for 25% of the time, Pallas kernels for 0%

profile of v1, /device:TPU:16, one launch (start us, length us, event | category | flops | bytes accessed | tf_op | source)
XLA Modules:
  0.0 135.7 jit_solution(4199759706810612827)
XLA Ops:
  0.6 1.2 copy.109
  1.8 1.1 copy.108
  2.9 1.1 copy.107
  4.2 1.1 copy.110
  5.3 11.0 %all-to-all-start = ((bf16[1,3,128,4,16,16]{2,5,3,1,0,4:T(8,128)(2,1)}), bf16[1,3,128,4,16,16]{2,5,3,1,0,4:T(8,128)(2,1)S(1)}, u32[]{:S(2)}, u32[]{:S(2)}) async-start(bf16[1,3,128,4,16,16]{2,5,3,1,0,4:T(8,128)(2,1)} %copy.110), calls=%async_computation | async-start | bytes 1572864 | tf_op jit(solution)/shard_map/all_to_all | solution.py:85
  21.3 19.6 %all-to-all-done = bf16[1,3,128,4,16,16]{2,5,3,1,0,4:T(8,128)(2,1)S(1)} async-done(((bf16[1,3,128,4,16,16]{2,5,3,1,0,4:T(8,128)(2,1)}), bf16[1,3,128,4,16,16]{2,5,3,1,0,4:T(8,128)(2,1)S(1)}, u32[]{:S(2)}, u32[]{:S(2)}) %all-to-all-start) | async-done | bytes 786464 | tf_op jit(solution)/shard_map/all_to_all | solution.py:85
  41.8 4.8 %all-to-all-start.2 = ((bf16[4,32,16,128]{3,2,1,0:T(8,128)(2,1)}), bf16[4,32,16,128]{3,2,1,0:T(8,128)(2,1)S(1)}, u32[]{:S(2)}, u32[]{:S(2)}) async-start(bf16[4,32,16,128]{3,2,1,0:T(8,128)(2,1)} %broadcast_in_dim.12), calls=%async_computation.2 | async-start | bytes 1048576 | tf_op jit(solution)/shard_map/all_to_all | solution.py:89
  46.9 3.3 %collective-permute-start = (bf16[3,2,64]{1,2,0:T(8,128)(2,1)S(1)}, bf16[3,2,64]{1,2,0:T(8,128)(2,1)S(1)}, u32[]{:S(2)}, u32[]{:S(2)}) collective-permute-start(bf16[3,2,64]{1,2,0:T(8,128)(2,1)S(1)} %slice.177), channel_id=1, source_target_pairs={{0,64},{64,128},{128,192},{1,65},{65,129},{129,193},{2,66},{66,130... | collective-permute-start | bytes 2312 | tf_op jit(solution)/shard_map/ppermute | solution.py:26
  51.0 1.9 %collective-permute-done = bf16[3,2,64]{1,2,0:T(8,128)(2,1)S(1)} collective-permute-done((bf16[3,2,64]{1,2,0:T(8,128)(2,1)S(1)}, bf16[3,2,64]{1,2,0:T(8,128)(2,1)S(1)}, u32[]{:S(2)}, u32[]{:S(2)}) %collective-permute-start) | collective-permute-done | bytes 800 | tf_op jit(solution)/shard_map/ppermute | solution.py:26
  54.0 4.2 %fusion.4 = f32[16,16,128,64]{2,3,1,0:T(8,128)S(1)} fusion(f32[16,128,64]{1,2,0:T(8,128)S(1)} %bitcast.129, f32[16,128,64]{1,2,0:T(8,128)S(1)} %multiply_exponential_fusion.1), kind=kOutput, calls=%fused_computation.5 | convolution fusion | flops 3223339008 | bytes 9437184 | tf_op jit(solution)/shard_map/ij,rkjc->rkic/dot_general | solution.py:49
  58.3 3.2 %copy-done = f32[16,16,128,64]{2,3,1,0:T(8,128)} copy-done((f32[16,16,128,64]{2,3,1,0:T(8,128)}, f32[16,16,128,64]{2,3,1,0:T(8,128)S(1)}, u32[]{:S(2)}) %copy-start) | copy-done | bytes 8388632
  61.5 5.5 %slice.201 = f32[16,16,1,64]{2,3,1,0:T(8,128)} slice(f32[16,16,128,64]{2,3,1,0:T(8,128)S(1)} %fusion.4), slice={[0:16], [0:16], [127:128], [0:64]} | slice | bytes 131072 | tf_op jit(solution)/shard_map/slice | solution.py:50
  67.0 5.4 %copy.139 = f32[16,16,1,64]{3,0,1,2:T(8,128)S(1)} copy(f32[16,16,1,64]{2,3,1,0:T(8,128)} %slice.201) | data formatting | bytes 131072 | tf_op jit(solution)/shard_map/squeeze | solution.py:50
  72.4 1.3 multiply_reduce_fusion.1
  74.4 3.7 %collective-permute-start.1 = (f32[16,64]{1,0:T(8,128)S(1)}, f32[16,64]{1,0:T(8,128)S(1)}, u32[]{:S(2)}, u32[]{:S(2)}) collective-permute-start(f32[16,64]{1,0:T(8,128)S(1)} %fusion.25), channel_id=1, source_target_pairs={{0,64},{64,128},{128,192},{1,65},{65,129},{129,193},{2,66},{66,130... | collective-permute-start | bytes 12296 | tf_op jit(solution)/shard_map/ppermute | solution.py:26
  78.1 1.3 collective-permute-start.2
  80.0 5.2 %collective-permute-done.2 = f32[16,64]{1,0:T(8,128)S(1)} collective-permute-done((f32[16,64]{1,0:T(8,128)S(1)}, f32[16,64]{1,0:T(8,128)S(1)}, u32[]{:S(2)}, u32[]{:S(2)}) %collective-permute-start.2) | collective-permute-done | bytes 4128 | tf_op jit(solution)/shard_map/ppermute | solution.py:26
  85.3 5.4 %multiply_reduce_fusion = f32[16,128,64]{1,2,0:T(8,128)S(1)} fusion(f32[16,16,128,64]{2,3,1,0:T(8,128)} %copy-done, f32[16,16,64]{2,1,0:T(8,128)S(1)} %multiply_add_fusion, f32[16,128,64]{1,2,0:T(8,128)S(1)} %get-tuple-element.42, f32[16,128,64]{1,2,0:T(8,128)S(1)} %get-tuple-element.41, f32[16,64]{1,0:T(8,128)S(1)} %get-tuple-element.38), kind=kLoop, calls=%fused_computation | loop fusion | flops 10354688 | bytes 10031104 | tf_op jit(solution)/shard_map/reduce_sum | solution.py:71
  91.9 1.9 %collective-permute-start.4 = (bf16[16,64]{0,1:T(8,128)(2,1)S(1)}, bf16[16,64]{0,1:T(8,128)(2,1)S(1)}, u32[]{:S(2)}, u32[]{:S(2)}) collective-permute-start(bf16[16,64]{0,1:T(8,128)(2,1)S(1)} %slice.205), channel_id=1, source_target_pairs={{64,0},{128,64},{192,128},{65,1},{129,65},{193,129},{66,2},{130,66... | collective-permute-start | bytes 6152 | tf_op jit(solution)/shard_map/ppermute | solution.py:26
  103.7 4.5 %all-to-all-start.3 = ((f32[16,8,128]{2,1,0:T(8,128)}), f32[16,8,128]{2,1,0:T(8,128)S(1)}, u32[]{:S(2)}, u32[]{:S(2)}) async-start(f32[16,8,128]{2,1,0:T(8,128)} %fusion.8), calls=%async_computation.3 | async-start | bytes 131072 | tf_op jit(solution)/shard_map/all_to_all | solution.py:127
  109.4 9.3 %all-to-all-done.3 = f32[16,8,128]{2,1,0:T(8,128)S(1)} async-done(((f32[16,8,128]{2,1,0:T(8,128)}), f32[16,8,128]{2,1,0:T(8,128)S(1)}, u32[]{:S(2)}, u32[]{:S(2)}) %all-to-all-start.3) | async-done | bytes 65568 | tf_op jit(solution)/shard_map/all_to_all | solution.py:127
  118.8 3.5 %all-to-all-start.1 = ((bf16[16,1,128,4,1,16]{2,5,4,3,1,0:T(8,128)(2,1)}), bf16[16,1,128,4,1,16]{2,5,4,3,1,0:T(8,128)(2,1)S(1)}, u32[]{:S(2)}, u32[]{:S(2)}) async-start(bf16[16,1,128,4,1,16]{2,5,4,3,1,0:T(8,128)(2,1)} %constant_dynamic-update-slice_fusion), calls=%async_computation.1 | async-start | bytes 524288 | tf_op jit(solution)/shard_map/all_to_all | solution.py:13
  123.6 6.1 %all-reduce = bf16[8,128]{1,0:T(8,128)(2,1)S(1)} all-reduce(f32[8,128]{1,0:T(8,128)S(1)} %reduce_sum.29), channel_id=2, replica_groups=mesh['u'=4,'v'=16,'tp'=4] {'tp'}, use_global_device_ids=true, to_apply=%region_3.4.clone | all-reduce | flops 1024 | bytes 6144
  130.2 4.7 %all-to-all-done.1 = bf16[16,1,128,4,1,16]{2,5,4,3,1,0:T(8,128)(2,1)S(1)} async-done(((bf16[16,1,128,4,1,16]{2,5,4,3,1,0:T(8,128)(2,1)}), bf16[16,1,128,4,1,16]{2,5,4,3,1,0:T(8,128)(2,1)S(1)}, u32[]{:S(2)}, u32[]{:S(2)}) %all-to-all-start.1) | async-done | bytes 262176 | tf_op jit(solution)/shard_map/all_to_all | solution.py:13
  (84 shorter events, 23.6 us)
Async XLA Ops:
  0.6 40.3 %copy-start.1 = (bf16[32,16,128]{2,1,0:T(8,128)(2,1)S(1)}, bf16[32,16,128]{2,1,0:T(8,128)(2,1)}, u32[]{:S(2)}) copy-start(bf16[32,16,128]{2,1,0:T(8,128)(2,1)} %param.15) | copy-start | bytes 393220
  5.3 35.6 %all-to-all-start = ((bf16[1,3,128,4,16,16]{2,5,3,1,0,4:T(8,128)(2,1)}), bf16[1,3,128,4,16,16]{2,5,3,1,0,4:T(8,128)(2,1)S(1)}, u32[]{:S(2)}, u32[]{:S(2)}) async-start(bf16[1,3,128,4,16,16]{2,5,3,1,0,4:T(8,128)(2,1)} %copy.110), calls=%async_computation | async-start | bytes 1572864 | tf_op jit(solution)/shard_map/all_to_all | solution.py:85
  41.8 37.7 %all-to-all-start.2 = ((bf16[4,32,16,128]{3,2,1,0:T(8,128)(2,1)}), bf16[4,32,16,128]{3,2,1,0:T(8,128)(2,1)S(1)}, u32[]{:S(2)}, u32[]{:S(2)}) async-start(bf16[4,32,16,128]{3,2,1,0:T(8,128)(2,1)} %broadcast_in_dim.12), calls=%async_computation.2 | async-start | bytes 1048576 | tf_op jit(solution)/shard_map/all_to_all | solution.py:89
  46.9 6.0 %collective-permute-start = (bf16[3,2,64]{1,2,0:T(8,128)(2,1)S(1)}, bf16[3,2,64]{1,2,0:T(8,128)(2,1)S(1)}, u32[]{:S(2)}, u32[]{:S(2)}) collective-permute-start(bf16[3,2,64]{1,2,0:T(8,128)(2,1)S(1)} %slice.177), channel_id=1, source_target_pairs={{0,64},{64,128},{128,192},{1,65},{65,129},{129,193},{2,66},{66,130... | collective-permute-start | bytes 2312 | tf_op jit(solution)/shard_map/ppermute | solution.py:26
  58.3 3.2 %copy-start = (f32[16,16,128,64]{2,3,1,0:T(8,128)}, f32[16,16,128,64]{2,3,1,0:T(8,128)S(1)}, u32[]{:S(2)}) copy-start(f32[16,16,128,64]{2,3,1,0:T(8,128)S(1)} %fusion.4) | copy-start | bytes 25165828
  73.8 5.8 %collective-permute-start.3 = (f32[16,64]{1,0:T(8,128)S(1)}, f32[16,64]{1,0:T(8,128)S(1)}, u32[]{:S(2)}, u32[]{:S(2)}) collective-permute-start(f32[16,64]{1,0:T(8,128)S(1)} %fusion.25), channel_id=1, source_target_pairs={{0,192},{1,193},{2,194},{3,195},{4,196},{5,197},{6,198},{7,199},{8... | collective-permute-start | bytes 12296 | tf_op jit(solution)/shard_map/ppermute | solution.py:26
  74.4 5.5 %collective-permute-start.1 = (f32[16,64]{1,0:T(8,128)S(1)}, f32[16,64]{1,0:T(8,128)S(1)}, u32[]{:S(2)}, u32[]{:S(2)}) collective-permute-start(f32[16,64]{1,0:T(8,128)S(1)} %fusion.25), channel_id=1, source_target_pairs={{0,64},{64,128},{128,192},{1,65},{65,129},{129,193},{2,66},{66,130... | collective-permute-start | bytes 12296 | tf_op jit(solution)/shard_map/ppermute | solution.py:26
  78.1 7.0 %collective-permute-start.2 = (f32[16,64]{1,0:T(8,128)S(1)}, f32[16,64]{1,0:T(8,128)S(1)}, u32[]{:S(2)}, u32[]{:S(2)}) collective-permute-start(f32[16,64]{1,0:T(8,128)S(1)} %fusion.25), channel_id=1, source_target_pairs={{0,128},{64,192},{1,129},{65,193},{2,130},{66,194},{3,131},{67,195... | collective-permute-start | bytes 12296 | tf_op jit(solution)/shard_map/ppermute | solution.py:26
  85.3 37.0 %copy-start.2 = (u32[256]{0:T(256)S(1)}, u32[256]{0:T(256)}, u32[]{:S(2)}) copy-start(u32[256]{0:T(256)} %constant.46) | copy-start | bytes 3076
  91.9 10.1 %collective-permute-start.4 = (bf16[16,64]{0,1:T(8,128)(2,1)S(1)}, bf16[16,64]{0,1:T(8,128)(2,1)S(1)}, u32[]{:S(2)}, u32[]{:S(2)}) collective-permute-start(bf16[16,64]{0,1:T(8,128)(2,1)S(1)} %slice.205), channel_id=1, source_target_pairs={{64,0},{128,64},{192,128},{65,1},{129,65},{193,129},{66,2},{130,66... | collective-permute-start | bytes 6152 | tf_op jit(solution)/shard_map/ppermute | solution.py:26
  103.7 15.1 %all-to-all-start.3 = ((f32[16,8,128]{2,1,0:T(8,128)}), f32[16,8,128]{2,1,0:T(8,128)S(1)}, u32[]{:S(2)}, u32[]{:S(2)}) async-start(f32[16,8,128]{2,1,0:T(8,128)} %fusion.8), calls=%async_computation.3 | async-start | bytes 131072 | tf_op jit(solution)/shard_map/all_to_all | solution.py:127
  118.8 16.1 %all-to-all-start.1 = ((bf16[16,1,128,4,1,16]{2,5,4,3,1,0:T(8,128)(2,1)}), bf16[16,1,128,4,1,16]{2,5,4,3,1,0:T(8,128)(2,1)S(1)}, u32[]{:S(2)}, u32[]{:S(2)}) async-start(bf16[16,1,128,4,1,16]{2,5,4,3,1,0:T(8,128)(2,1)} %constant_dynamic-update-slice_fusion), calls=%async_computation.1 | async-start | bytes 524288 | tf_op jit(solution)/shard_map/all_to_all | solution.py:13
